TPU v7x, 32 devices: a whole 2x2x4 slice. The times are simulated.
32 devices in a mesh: grp: 2 (over y), dev: 16 (over z, x, core).
Axes of the slice: x: 2, y: 2, z: 4, core: 2. Of those that a mesh axis runs over, the one named last changes fastest.
Arguments:
- sources: bfloat16 [65536, 768], P(('grp', 'dev')), may hold values from -6 to 6
- encoder: bfloat16 [65536, 256], P(('grp', 'dev')), may hold values from -0.125 to 0.125
- section_weight: bfloat16 [32, 4, 2, 256, 256], P(('grp', 'dev')), may hold values from -0.25 to 0.25
- cross_weight: bfloat16 [2, 16, 2, 256, 256], P('grp', 'dev'), may hold values from -0.25 to 0.25
- local_weight: bfloat16 [32, 14, 256, 256], P(('grp', 'dev')), may hold values from -0.375 to 0.375
- decoder: bfloat16 [65536, 256], P(('grp', 'dev')), may hold values from -0.375 to 0.375
Outputs:
- target_values: bfloat16 [65536, 768], P(('grp', 'dev'))
All inputs are finite; a program needn't handle non-finite values.
Results may differ from a plain program's by a relative error of at most 0.02.
Values may be sent and summed in bfloat16 or wider, within the bound.
No kernel may reach another device: no remote copies, remote signals or barrier semaphores. Data moves between devices by JAX's collectives and lax.ppermute only.
A program may use at most 64 MiB of HBM per device.

v0:
```python
import functools

import jax
import jax.numpy as jnp
from jax import lax
from jax.experimental import pallas as pl
from jax.experimental.pallas import tpu as pltpu
from jax.sharding import PartitionSpec as P

LEVELS = 3
F32 = jnp.float32
BF16 = jnp.bfloat16
VMEM = pl.BlockSpec(memory_space=pltpu.VMEM)
HBM = pl.BlockSpec(memory_space=pltpu.HBM)
MIB = 1 << 20
PARTS = 2


def dot(a, b):
    return jnp.dot(a, b, preferred_element_type=F32)


def dot_first(a, b):
    return lax.dot_general(a, b, (((0,), (0,)), ((), ())), preferred_element_type=F32)


def cost(flops, moved):
    return pl.CostEstimate(flops=flops, bytes_accessed=moved, transcendentals=0)


def pieces_of(columns, shares):
    edges = [0]
    for share in shares:
        edges.append(edges[-1] + columns * share // sum(shares))
    return list(zip(edges[:-1], edges[1:]))


def partitions(columns, sections):
    first, near, far, long, last = SHARES
    shares = [first, near] + [far] * (sections - 3) + [long, last]
    return [pieces_of(columns, share) for share in shares]


def head_kernel(pieces, encoder_hbm, sources_hbm, first_ref, encoder_ref, *refs):
    near, sems = [refs[-2], *refs[:-2]], refs[-1]
    rows = encoder_ref.shape[0] // PARTS
    spans = [pl.ds(part * rows, rows) for part in range(PARTS)]

    def fetch(source, target, sem):
        copy = pltpu.make_async_copy(source, target, sem)
        copy.start()
        return copy

    lo, hi = pieces[0]
    early = []
    for part, span in enumerate(spans):
        early.append(fetch(encoder_hbm.at[span, :], encoder_ref.at[span, :], sems.at[0, part]))
        early.append(fetch(sources_hbm.at[span, pl.ds(lo, hi - lo)], near[0].at[span, :], sems.at[1, part]))
    later = [
        fetch(sources_hbm.at[:, pl.ds(lo, hi - lo)], near[i].at[:, :], sems.at[2, i])
        for i, (lo, hi) in enumerate(pieces)
        if i
    ]
    total = None
    for part, span in enumerate(spans):
        early[2 * part].wait()
        early[2 * part + 1].wait()
        term = dot_first(encoder_ref[span, :], near[0][span, :])
        total = term if total is None else total + term
    first_ref[...] = total.astype(BF16)
    for copy in later:
        copy.wait()


def encode_head(encoder, sources, pieces):
    points, size = encoder.shape
    columns = sources.shape[1]
    widths = [hi - lo for lo, hi in pieces]
    return pl.pallas_call(
        functools.partial(head_kernel, pieces),
        out_shape=[
            jax.ShapeDtypeStruct((size, widths[0]), BF16),
            jax.ShapeDtypeStruct((points, size), BF16),
            *[jax.ShapeDtypeStruct((points, width), BF16) for width in widths[1:]],
        ],
        in_specs=[HBM, HBM],
        out_specs=[VMEM] * (1 + len(widths)),
        scratch_shapes=[
            pltpu.VMEM((points, widths[0]), BF16),
            pltpu.SemaphoreType.DMA((3, max(PARTS, len(pieces)))),
        ],
        compiler_params=pltpu.CompilerParams(vmem_limit_bytes=24 * MIB),
        cost_estimate=cost(2 * points * size * widths[0], 2 * points * (size + columns)),
        name="head",
    )(
        pltpu.with_memory_space_constraint(encoder, pltpu.HBM),
        pltpu.with_memory_space_constraint(sources, pltpu.HBM),
    )


def piece_kernel(encoder_ref, sources_ref, out_ref):
    out_ref[...] = dot_first(encoder_ref[...], sources_ref[...]).astype(BF16)


def encode_piece(encoder, sources):
    points, size = encoder.shape
    width = sources.shape[1]
    return pl.pallas_call(
        piece_kernel,
        out_shape=jax.ShapeDtypeStruct((size, width), BF16),
        in_specs=[VMEM] * 2,
        out_specs=VMEM,
        compiler_params=pltpu.CompilerParams(vmem_limit_bytes=8 * MIB),
        cost_estimate=cost(2 * points * size * width, 2 * points * width),
        name="encode",
    )(encoder, sources)


def overlaps(piece, earlier):
    lo, hi = piece
    return [i for i, (a, b) in enumerate(earlier) if a < hi and b > lo]


def section_kernel(bit, piece, earlier, weight_ref, *refs):
    out_ref = refs[-1]
    lo, hi = piece
    for i, (a, b) in enumerate(earlier):
        own_ref, other_ref = refs[2 * i], refs[2 * i + 1]
        start, stop = max(a, lo), min(b, hi)
        cols = slice(start - a, stop - a)
        out_ref[:, start - lo : stop - lo] = (
            dot(weight_ref[0, bit, 0], own_ref[:, cols]) + dot(weight_ref[0, bit, 1], other_ref[:, cols])
        ).astype(BF16)


def section(weights, bit, piece, earlier, boxes):
    size = weights.shape[-1]
    width = piece[1] - piece[0]
    return pl.pallas_call(
        functools.partial(section_kernel, bit, piece, earlier),
        out_shape=jax.ShapeDtypeStruct((size, width), BF16),
        in_specs=[VMEM] * (1 + len(boxes)),
        out_specs=VMEM,
        compiler_params=pltpu.CompilerParams(vmem_limit_bytes=8 * MIB),
        cost_estimate=cost(4 * size * size * width, 1 * MIB),
        name="section",
    )(weights, *boxes)


def operator_kernel(weight_ref, decoder_ref, out_ref):
    leaf = decoder_ref.shape[0] // 2**LEVELS
    chain = [weight_ref[0, 0], weight_ref[0, 1]]
    offset = 2
    for level in range(1, LEVELS):
        children = 2 ** (level + 1)
        chain = [dot(weight_ref[0, offset + c], chain[c // 2]).astype(BF16) for c in range(children)]
        offset += children
    for c in range(2**LEVELS):
        rows = slice(c * leaf, (c + 1) * leaf)
        out_ref[rows, :] = dot(decoder_ref[rows, :], chain[c]).astype(BF16)


def local_operator(local_weight, decoder):
    points, size = decoder.shape
    return pl.pallas_call(
        operator_kernel,
        out_shape=jax.ShapeDtypeStruct((points, size), BF16),
        in_specs=[VMEM] * 2,
        out_specs=VMEM,
        compiler_params=pltpu.CompilerParams(vmem_limit_bytes=12 * MIB),
        cost_estimate=cost(2 * 20 * size**3, 4 * MIB),
        name="operator",
    )(local_weight, decoder)


TAIL_STEPS = 4


def finish_kernel(count, piece, held_piece, crossing_ref, *refs):
    boxes, operator_ref = refs[:count], refs[count]
    out_hbm, staged_ref, sems = refs[-3:]
    copies = []

    def store(source, rows, piece, sem):
        lo, hi = piece
        copies.append(pltpu.make_async_copy(source, out_hbm.at[rows, pl.ds(lo, hi - lo)], sem))
        copies[-1].start()

    if held_piece is not None:
        store(refs[count + 1], pl.ds(0, operator_ref.shape[0]), held_piece, sems.at[TAIL_STEPS])
    merged = merge(crossing_ref, boxes)
    rows = operator_ref.shape[0] // TAIL_STEPS
    for step in range(TAIL_STEPS):
        span = pl.ds(step * rows, rows)
        staged_ref[span, :] = dot(operator_ref[span, :], merged).astype(BF16)
        store(staged_ref.at[span, :], span, piece, sems.at[step])
    for copy in copies:
        copy.wait()


def merge(crossing_ref, boxes):
    total = dot(crossing_ref[0], boxes[0][...])
    for h in range(1, len(boxes)):
        total = total + dot(crossing_ref[h], boxes[h][...])
    return total.astype(BF16)


def hold_kernel(count, crossing_ref, *refs):
    refs[-1][...] = dot(refs[count][...], merge(crossing_ref, refs[:count])).astype(BF16)


def hold(crossing, boxes, operator):
    points, size = operator.shape
    width = boxes[0].shape[1]
    return pl.pallas_call(
        functools.partial(hold_kernel, len(boxes)),
        out_shape=jax.ShapeDtypeStruct((points, width), BF16),
        in_specs=[VMEM] * (2 + len(boxes)),
        out_specs=VMEM,
        compiler_params=pltpu.CompilerParams(vmem_limit_bytes=12 * MIB),
        cost_estimate=cost(2 * points * size * width, 2 * points * width),
        name="hold",
    )(crossing, *boxes, operator)


def finish(crossing, boxes, operator, piece, columns, prior, held=None, held_piece=None):
    points, size = operator.shape
    lo, hi = piece
    width = hi - lo
    operands = [crossing, *boxes, operator]
    if held is not None:
        operands.append(held)
    in_specs = [VMEM] * len(operands)
    aliases = {}
    if prior is not None:
        aliases = {len(operands): 0}
        operands.append(prior)
        in_specs.append(HBM)
    return pl.pallas_call(
        functools.partial(finish_kernel, len(boxes), piece, held_piece),
        out_shape=jax.ShapeDtypeStruct((points, columns), BF16),
        in_specs=in_specs,
        out_specs=HBM,
        scratch_shapes=[pltpu.VMEM((points, width), BF16), pltpu.SemaphoreType.DMA((TAIL_STEPS + 1,))],
        input_output_aliases=aliases,
        compiler_params=pltpu.CompilerParams(vmem_limit_bytes=12 * MIB),
        cost_estimate=cost(2 * points * size * width, 2 * points * width),
        name="finish",
    )(*operands)


def from_partner(block, axis, bit):
    count = lax.axis_size(axis)
    block = pltpu.with_memory_space_constraint(block, pltpu.VMEM)
    other = lax.ppermute(block, axis, [(i, i ^ (1 << bit)) for i in range(count)])
    return pltpu.with_memory_space_constraint(other, pltpu.VMEM)


def shards(sources, encoder, section_weight, cross_weight, local_weight, decoder):
    sections = lax.axis_size("dev").bit_length() - 1
    groups = lax.axis_size("grp")
    columns = sources.shape[1]
    plan = partitions(columns, sections)
    operator = local_operator(local_weight, decoder)
    crossing = cross_weight[0, 0]
    if groups == 2:
        me = lax.axis_index("grp")
        crossing = jnp.stack([crossing[me], crossing[1 - me]])
    first, encoder_near, *near = encode_head(encoder, sources, plan[0])
    coeffs = [first]
    for block in near:
        coeffs.append(encode_piece(encoder_near, block))
    for stage in range(sections):
        others = []
        for block in coeffs:
            others.append(from_partner(block, "dev", stage))
        mixed = []
        for piece in plan[stage + 1]:
            used = overlaps(piece, plan[stage])
            boxes = [box for j in used for box in (coeffs[j], others[j])]
            mixed.append(
                section(section_weight, stage, piece, [plan[stage][j] for j in used], boxes)
            )
        coeffs = mixed
    out = None
    arrived = []
    for block in coeffs:
        if groups == 2:
            arrived.append([block, from_partner(block, "grp", 0)])
        else:
            every = lax.all_gather(block, "grp")
            arrived.append([every[h] for h in range(groups)])
    held = held_piece = None
    for i, (piece, boxes) in enumerate(zip(plan[sections], arrived)):
        if i and i == len(arrived) - 2:
            held, held_piece = hold(crossing, boxes, operator), piece
        else:
            out = finish(crossing, boxes, operator, piece, columns, out, held, held_piece)
    return out


SHARES = ((1, 5), (1, 2, 3), (1, 2, 2, 1), (1, 2, 2, 1), (1, 2, 2, 1))


def solution(mesh):
    placed = (
        P(("grp", "dev"), None),
        P(("grp", "dev"), None),
        P(("grp", "dev"), None, None, None, None),
        P("grp", "dev", None, None, None),
        P(("grp", "dev"), None, None, None),
        P(("grp", "dev"), None),
    )
    return jax.shard_map(
        shards, mesh=mesh, in_specs=placed, out_specs=P(("grp", "dev"), None), check_vma=False
    )
```

profile of v0, /device:TPU:0, one launch (start us, length us, event | category | flops | bytes accessed | tf_op | source)
XLA Modules:
  0.0 54.6 jit_solution(4684250376524749256)
XLA Ops:
  0.0 0.0 copy-start
  0.0 2.4 %head.1 = (bf16[256,128]{1,0:T(8,128)(2,1)S(1)}, bf16[2048,256]{1,0:T(8,128)(2,1)S(1)}, bf16[2048,640]{1,0:T(8,128)(2,1)S(1)}) custom-call(bf16[2048,256]{1,0:T(8,128)(2,1)} %encoder_hbm.1, bf16[2048,768]{1,0:T(8,128)(2,1)} %sources_hbm.1), custom_call_target="tpu_custom_call" | custom-call | flops 134217728 | bytes 4194304 | tf_op jit(solution)/shard_map/head/pallas_call | solution.py:79
  2.4 1.0 %encode.1.refs_0_ = bf16[256,640]{1,0:T(8,128)(2,1)S(1)} custom-call(bf16[2048,256]{1,0:T(8,128)(2,1)S(1)} %get-tuple-element.8.encoder_ref, bf16[2048,640]{1,0:T(8,128)(2,1)S(1)} %get-tuple-element.9.sources_ref), custom_call_target="tpu_custom_call" | custom-call | flops 671088640 | bytes 2621440 | tf_op jit(solution)/shard_map/encode/pallas_call | solution.py:108
  3.4 0.6 %collective-permute-start = (bf16[256,640]{1,0:T(8,128)(2,1)S(1)}, bf16[256,640]{1,0:T(8,128)(2,1)S(1)}, u32[]{:S(2)}, u32[]{:S(2)}) collective-permute-start(bf16[256,640]{1,0:T(8,128)(2,1)S(1)} %encode.1.refs_0_), channel_id=1, source_target_pairs={{0,1},{1,0},{2,3},{3,2},{4,5},{5,4},{6,7},{7,6},{8,9},{9,8},{10,11... | collective-permute-start | bytes 983048 | tf_op jit(solution)/shard_map/ppermute | solution.py:255
  4.0 1.3 %collective-permute-done.refs_1_ = bf16[256,640]{1,0:T(8,128)(2,1)S(1)} collective-permute-done((bf16[256,640]{1,0:T(8,128)(2,1)S(1)}, bf16[256,640]{1,0:T(8,128)(2,1)S(1)}, u32[]{:S(2)}, u32[]{:S(2)}) %collective-permute-start) | collective-permute-done | bytes 327712 | tf_op jit(solution)/shard_map/ppermute | solution.py:255
  5.2 0.0 copy-done
  5.2 0.3 section.15.refs_0_
  5.5 2.9 %collective-permute-start.1 = (bf16[256,384]{1,0:T(8,128)(2,1)S(1)}, bf16[256,384]{1,0:T(8,128)(2,1)S(1)}, u32[]{:S(2)}, u32[]{:S(2)}) collective-permute-start(bf16[256,384]{1,0:T(8,128)(2,1)S(1)} %section.15.refs_0_), channel_id=1, source_target_pairs={{0,2},{1,3},{2,0},{3,1},{4,6},{5,7},{6,4},{7,5},{8,10},{9,11},{10,... | collective-permute-start | bytes 589832 | tf_op jit(solution)/shard_map/ppermute | solution.py:255
  8.4 0.2 section.22.refs_0_
  8.7 0.1 collective-permute-start.8
  8.7 0.1 collective-permute-start.12
  8.8 7.6 %collective-permute-done.8.refs_1_ = bf16[256,256]{1,0:T(8,128)(2,1)S(1)} collective-permute-done((bf16[256,256]{1,0:T(8,128)(2,1)S(1)}, bf16[256,256]{1,0:T(8,128)(2,1)S(1)}, u32[]{:S(2)}, u32[]{:S(2)}) %collective-permute-start.8) | collective-permute-done | bytes 131104 | tf_op jit(solution)/shard_map/ppermute | solution.py:255
  16.4 0.2 section.23.refs_0_
  16.7 1.9 %collective-permute-start.9 = (bf16[256,256]{1,0:T(8,128)(2,1)S(1)}, bf16[256,256]{1,0:T(8,128)(2,1)S(1)}, u32[]{:S(2)}, u32[]{:S(2)}) collective-permute-start(bf16[256,256]{1,0:T(8,128)(2,1)S(1)} %section.23.refs_0_), channel_id=1, source_target_pairs={{0,4},{1,5},{2,6},{3,7},{4,0},{5,1},{6,2},{7,3},{8,12},{9,13},{10,... | collective-permute-start | bytes 393224 | tf_op jit(solution)/shard_map/ppermute | solution.py:255
  18.6 0.0 collective-permute-done.1.refs_1_
  18.6 0.2 section.19.refs_0_
  18.8 0.0 copy-start.3
  18.8 0.3 collective-permute-start.5
  19.1 0.0 collective-permute-done.12.refs_1_
  19.1 0.2 section.26.refs_0_
  19.3 1.8 %collective-permute-start.13 = (bf16[256,128]{1,0:T(8,128)(2,1)S(1)}, bf16[256,128]{1,0:T(8,128)(2,1)S(1)}, u32[]{:S(2)}, u32[]{:S(2)}) collective-permute-start(bf16[256,128]{1,0:T(8,128)(2,1)S(1)} %section.26.refs_0_), channel_id=1, source_target_pairs={{0,2},{1,3},{2,0},{3,1},{4,6},{5,7},{6,4},{7,5},{8,10},{9,11},{10,... | collective-permute-start | bytes 196616 | tf_op jit(solution)/shard_map/ppermute | solution.py:255
  21.1 2.5 %collective-permute-done.13.refs_1_ = bf16[256,128]{1,0:T(8,128)(2,1)S(1)} collective-permute-done((bf16[256,128]{1,0:T(8,128)(2,1)S(1)}, bf16[256,128]{1,0:T(8,128)(2,1)S(1)}, u32[]{:S(2)}, u32[]{:S(2)}) %collective-permute-start.13) | collective-permute-done | bytes 65568 | tf_op jit(solution)/shard_map/ppermute | solution.py:255
  23.6 0.2 section.27.refs_0_
  23.9 1.9 %collective-permute-start.14 = (bf16[256,128]{1,0:T(8,128)(2,1)S(1)}, bf16[256,128]{1,0:T(8,128)(2,1)S(1)}, u32[]{:S(2)}, u32[]{:S(2)}) collective-permute-start(bf16[256,128]{1,0:T(8,128)(2,1)S(1)} %section.27.refs_0_), channel_id=1, source_target_pairs={{0,4},{1,5},{2,6},{3,7},{4,0},{5,1},{6,2},{7,3},{8,12},{9,13},{10,... | collective-permute-start | bytes 196616 | tf_op jit(solution)/shard_map/ppermute | solution.py:255
  25.7 0.2 section.16.refs_0_
  25.9 0.3 collective-permute-start.2
  26.2 0.0 collective-permute-done.9.refs_1_
  26.2 0.2 section.24.refs_0_
  26.5 2.9 %collective-permute-start.10 = (bf16[256,256]{1,0:T(8,128)(2,1)S(1)}, bf16[256,256]{1,0:T(8,128)(2,1)S(1)}, u32[]{:S(2)}, u32[]{:S(2)}) collective-permute-start(bf16[256,256]{1,0:T(8,128)(2,1)S(1)} %section.24.refs_0_), channel_id=1, source_target_pairs={{0,8},{1,9},{2,10},{3,11},{4,12},{5,13},{6,14},{7,15},{8,0},{9,1},... | collective-permute-start | bytes 393224 | tf_op jit(solution)/shard_map/ppermute | solution.py:255
  29.4 0.0 collective-permute-done.5.refs_1_
  29.4 0.2 section.20.refs_0_
  29.6 0.2 collective-permute-start.6
  29.7 0.0 copy-done.3
  29.8 0.0 collective-permute-done.14.refs_1_
  29.8 0.2 section.28.refs_0_
  30.0 2.9 %collective-permute-start.15 = (bf16[256,128]{1,0:T(8,128)(2,1)S(1)}, bf16[256,128]{1,0:T(8,128)(2,1)S(1)}, u32[]{:S(2)}, u32[]{:S(2)}) collective-permute-start(bf16[256,128]{1,0:T(8,128)(2,1)S(1)} %section.28.refs_0_), channel_id=1, source_target_pairs={{0,8},{1,9},{2,10},{3,11},{4,12},{5,13},{6,14},{7,15},{8,0},{9,1},... | collective-permute-start | bytes 196616 | tf_op jit(solution)/shard_map/ppermute | solution.py:255
  32.9 0.0 collective-permute-done.2.refs_1_
  32.9 0.2 section.17.refs_0_
  33.1 0.0 copy-start.1
  33.1 0.0 copy-start.2
  33.1 0.7 %collective-permute-start.3 = (bf16[256,128]{1,0:T(8,128)(2,1)S(1)}, bf16[256,128]{1,0:T(8,128)(2,1)S(1)}, u32[]{:S(2)}, u32[]{:S(2)}) collective-permute-start(bf16[256,128]{1,0:T(8,128)(2,1)S(1)} %section.17.refs_0_), channel_id=1, source_target_pairs={{0,8},{1,9},{2,10},{3,11},{4,12},{5,13},{6,14},{7,15},{8,0},{9,1},... | collective-permute-start | bytes 196616 | tf_op jit(solution)/shard_map/ppermute | solution.py:255
  33.9 6.9 %collective-permute-done.10.refs_1_ = bf16[256,256]{1,0:T(8,128)(2,1)S(1)} collective-permute-done((bf16[256,256]{1,0:T(8,128)(2,1)S(1)}, bf16[256,256]{1,0:T(8,128)(2,1)S(1)}, u32[]{:S(2)}, u32[]{:S(2)}) %collective-permute-start.10) | collective-permute-done | bytes 131104 | tf_op jit(solution)/shard_map/ppermute | solution.py:255
  40.8 0.2 section.25.refs_0_
  41.0 1.8 %collective-permute-start.11 = (bf16[256,256]{1,0:T(8,128)(2,1)S(1)}, bf16[256,256]{1,0:T(8,128)(2,1)S(1)}, u32[]{:S(2)}, u32[]{:S(2)}) collective-permute-start(bf16[256,256]{1,0:T(8,128)(2,1)S(1)} %section.25.refs_0_), channel_id=1, source_target_pairs={{0,16},{16,0},{1,17},{17,1},{2,18},{18,2},{3,19},{19,3},{4,20},{20... | collective-permute-start | bytes 393224 | tf_op jit(solution)/shard_map/ppermute | solution.py:255
  42.8 0.3 collective-permute-done.6.refs_1_
  43.2 0.2 section.21.refs_0_
  43.4 1.6 %collective-permute-start.7 = (bf16[256,256]{1,0:T(8,128)(2,1)S(1)}, bf16[256,256]{1,0:T(8,128)(2,1)S(1)}, u32[]{:S(2)}, u32[]{:S(2)}) collective-permute-start(bf16[256,256]{1,0:T(8,128)(2,1)S(1)} %section.21.refs_0_), channel_id=1, source_target_pairs={{0,16},{16,0},{1,17},{17,1},{2,18},{18,2},{3,19},{19,3},{4,20},{20... | collective-permute-start | bytes 393224 | tf_op jit(solution)/shard_map/ppermute | solution.py:255
  45.0 0.0 collective-permute-done.15.refs_1_
  45.0 0.2 section.29.refs_0_
  45.3 0.6 %collective-permute-start.16 = (bf16[256,128]{1,0:T(8,128)(2,1)S(1)}, bf16[256,128]{1,0:T(8,128)(2,1)S(1)}, u32[]{:S(2)}, u32[]{:S(2)}) collective-permute-start(bf16[256,128]{1,0:T(8,128)(2,1)S(1)} %section.29.refs_0_), channel_id=1, source_target_pairs={{0,16},{16,0},{1,17},{17,1},{2,18},{18,2},{3,19},{19,3},{4,20},{20... | collective-permute-start | bytes 196616 | tf_op jit(solution)/shard_map/ppermute | solution.py:255
  45.8 0.0 collective-permute-done.3.refs_1_
  45.8 0.2 section.18.refs_0_
  46.0 1.6 %collective-permute-start.4 = (bf16[256,128]{1,0:T(8,128)(2,1)S(1)}, bf16[256,128]{1,0:T(8,128)(2,1)S(1)}, u32[]{:S(2)}, u32[]{:S(2)}) collective-permute-start(bf16[256,128]{1,0:T(8,128)(2,1)S(1)} %section.18.refs_0_), channel_id=1, source_target_pairs={{0,16},{16,0},{1,17},{17,1},{2,18},{18,2},{3,19},{19,3},{4,20},{20... | collective-permute-start | bytes 196616 | tf_op jit(solution)/shard_map/ppermute | solution.py:255
  47.6 0.0 copy-done.1
  47.6 0.0 copy-done.2
  47.6 0.9 %operator.1.refs_2_ = bf16[2048,256]{1,0:T(8,128)(2,1)S(1)} custom-call(bf16[1,14,256,256]{3,2,1,0:T(8,128)(2,1)S(1)} %copy-done.1, bf16[2048,256]{1,0:T(8,128)(2,1)S(1)} %copy-done.2), custom_call_target="tpu_custom_call" | custom-call | flops 671088640 | bytes 4194304 | tf_op jit(solution)/shard_map/operator/pallas_call | solution.py:165
  48.6 1.0 %collective-permute-done.16.refs_1_ = bf16[256,128]{1,0:T(8,128)(2,1)S(1)} collective-permute-done((bf16[256,128]{1,0:T(8,128)(2,1)S(1)}, bf16[256,128]{1,0:T(8,128)(2,1)S(1)}, u32[]{:S(2)}, u32[]{:S(2)}) %collective-permute-start.16) | collective-permute-done | bytes 65568 | tf_op jit(solution)/shard_map/ppermute | solution.py:255
  49.6 1.4 %finish.3.refs_3_ = bf16[2048,768]{1,0:T(8,128)(2,1)} custom-call(bf16[2,256,256]{2,1,0:T(8,128)(2,1)S(1)} %pad_maximum_fusion.crossing_ref, bf16[256,128]{1,0:T(8,128)(2,1)S(1)} %section.29.refs_0_, bf16[256,128]{1,0:T(8,128)(2,1)S(1)} %collective-permute-done.16.refs_1_, bf16[2048,256]{1,0:T(8,128)(2,1)S(1)} %operator.1.refs_2_), custom_call_target="tpu_custom_call" | custom-call | flops 134217728 | bytes 524288 | tf_op jit(solution)/shard_map/finish/pallas_call | solution.py:239
  51.0 0.0 collective-permute-done.11.refs_1_
  51.0 1.5 %finish.4.refs_4_ = bf16[2048,768]{1,0:T(8,128)(2,1)} custom-call(bf16[2,256,256]{2,1,0:T(8,128)(2,1)S(1)} %pad_maximum_fusion.crossing_ref, bf16[256,256]{1,0:T(8,128)(2,1)S(1)} %section.25.refs_0_, bf16[256,256]{1,0:T(8,128)(2,1)S(1)} %collective-permute-done.11.refs_1_, bf16[2048,256]{1,0:T(8,128)(2,1)S(1)} %operator.1.refs_2_, ...), custom_call_target="tpu_custom_call", output_to_operand_aliasing={{}: (4, {})} | custom-call | flops 268435456 | bytes 1048576 | tf_op jit(solution)/shard_map/finish/pallas_call | solution.py:239
  52.5 0.0 collective-permute-done.7.refs_1_
  52.5 0.7 %hold.1.refs_3_ = bf16[2048,256]{1,0:T(8,128)(2,1)S(1)} custom-call(bf16[2,256,256]{2,1,0:T(8,128)(2,1)S(1)} %pad_maximum_fusion.crossing_ref, bf16[256,256]{1,0:T(8,128)(2,1)S(1)} %section.21.refs_0_, bf16[256,256]{1,0:T(8,128)(2,1)S(1)} %collective-permute-done.7.refs_1_, bf16[2048,256]{1,0:T(8,128)(2,1)S(1)} %operator.1.refs_2_), custom_call_target="tpu_custom_call" | custom-call | flops 268435456 | bytes 1048576 | tf_op jit(solution)/shard_map/hold/pallas_call | solution.py:215
  53.3 0.0 collective-permute-done.4.refs_1_
  53.3 1.4 %finish.5 = bf16[2048,768]{1,0:T(8,128)(2,1)} custom-call(bf16[2,256,256]{2,1,0:T(8,128)(2,1)S(1)} %pad_maximum_fusion.crossing_ref, bf16[256,128]{1,0:T(8,128)(2,1)S(1)} %section.18.refs_0_, bf16[256,128]{1,0:T(8,128)(2,1)S(1)} %collective-permute-done.4.refs_1_, bf16[2048,256]{1,0:T(8,128)(2,1)S(1)} %operator.1.refs_2_, ...), custom_call_target="tpu_custom_call", output_to_operand_aliasing={{}: (5, {})} | custom-call | flops 134217728 | bytes 524288 | tf_op jit(solution)/shard_map/finish/pallas_call | solution.py:239
  (2 shorter events, 0.0 us)
Async XLA Ops:
  0.0 5.2 %copy-start = (bf16[1,4,2,256,256]{4,3,2,1,0:T(8,128)(2,1)S(1)}, bf16[1,4,2,256,256]{4,3,2,1,0:T(8,128)(2,1)}, u32[]{:S(2)}) copy-start(bf16[1,4,2,256,256]{4,3,2,1,0:T(8,128)(2,1)} %weight_ref.31) | copy-start | bytes 3145732
  3.4 1.8 %collective-permute-start = (bf16[256,640]{1,0:T(8,128)(2,1)S(1)}, bf16[256,640]{1,0:T(8,128)(2,1)S(1)}, u32[]{:S(2)}, u32[]{:S(2)}) collective-permute-start(bf16[256,640]{1,0:T(8,128)(2,1)S(1)} %encode.1.refs_0_), channel_id=1, source_target_pairs={{0,1},{1,0},{2,3},{3,2},{4,5},{5,4},{6,7},{7,6},{8,9},{9,8},{10,11... | collective-permute-start | bytes 983048 | tf_op jit(solution)/shard_map/ppermute | solution.py:255
  5.5 13.0 %collective-permute-start.1 = (bf16[256,384]{1,0:T(8,128)(2,1)S(1)}, bf16[256,384]{1,0:T(8,128)(2,1)S(1)}, u32[]{:S(2)}, u32[]{:S(2)}) collective-permute-start(bf16[256,384]{1,0:T(8,128)(2,1)S(1)} %section.15.refs_0_), channel_id=1, source_target_pairs={{0,2},{1,3},{2,0},{3,1},{4,6},{5,7},{6,4},{7,5},{8,10},{9,11},{10,... | collective-permute-start | bytes 589832 | tf_op jit(solution)/shard_map/ppermute | solution.py:255
  8.7 7.8 %collective-permute-start.8 = (bf16[256,256]{1,0:T(8,128)(2,1)S(1)}, bf16[256,256]{1,0:T(8,128)(2,1)S(1)}, u32[]{:S(2)}, u32[]{:S(2)}) collective-permute-start(bf16[256,256]{1,0:T(8,128)(2,1)S(1)} %section.22.refs_0_), channel_id=1, source_target_pairs={{0,2},{1,3},{2,0},{3,1},{4,6},{5,7},{6,4},{7,5},{8,10},{9,11},{10,... | collective-permute-start | bytes 393224 | tf_op jit(solution)/shard_map/ppermute | solution.py:255
  8.7 10.3 %collective-permute-start.12 = (bf16[256,128]{1,0:T(8,128)(2,1)S(1)}, bf16[256,128]{1,0:T(8,128)(2,1)S(1)}, u32[]{:S(2)}, u32[]{:S(2)}) collective-permute-start(bf16[256,128]{1,0:T(8,128)(2,1)S(1)} %get-tuple-element.10.refs_0_), channel_id=1, source_target_pairs={{0,1},{1,0},{2,3},{3,2},{4,5},{5,4},{6,7},{7,6},{8,9},{9,8},{10,11... | collective-permute-start | bytes 196616 | tf_op jit(solution)/shard_map/ppermute | solution.py:255
  16.7 9.6 %collective-permute-start.9 = (bf16[256,256]{1,0:T(8,128)(2,1)S(1)}, bf16[256,256]{1,0:T(8,128)(2,1)S(1)}, u32[]{:S(2)}, u32[]{:S(2)}) collective-permute-start(bf16[256,256]{1,0:T(8,128)(2,1)S(1)} %section.23.refs_0_), channel_id=1, source_target_pairs={{0,4},{1,5},{2,6},{3,7},{4,0},{5,1},{6,2},{7,3},{8,12},{9,13},{10,... | collective-permute-start | bytes 393224 | tf_op jit(solution)/shard_map/ppermute | solution.py:255
  18.8 11.0 %copy-start.3 = (bf16[1,1,2,256,256]{4,3,2,1,0:T(8,128)(2,1)S(1)}, bf16[1,1,2,256,256]{4,3,2,1,0:T(8,128)(2,1)}, u32[]{:S(2)}) copy-start(bf16[1,1,2,256,256]{4,3,2,1,0:T(8,128)(2,1)} %param.9) | copy-start | bytes 786436
  18.8 10.6 %collective-permute-start.5 = (bf16[256,256]{1,0:T(8,128)(2,1)S(1)}, bf16[256,256]{1,0:T(8,128)(2,1)S(1)}, u32[]{:S(2)}, u32[]{:S(2)}) collective-permute-start(bf16[256,256]{1,0:T(8,128)(2,1)S(1)} %section.19.refs_0_), channel_id=1, source_target_pairs={{0,4},{1,5},{2,6},{3,7},{4,0},{5,1},{6,2},{7,3},{8,12},{9,13},{10,... | collective-permute-start | bytes 393224 | tf_op jit(solution)/shard_map/ppermute | solution.py:255
  19.3 4.3 %collective-permute-start.13 = (bf16[256,128]{1,0:T(8,128)(2,1)S(1)}, bf16[256,128]{1,0:T(8,128)(2,1)S(1)}, u32[]{:S(2)}, u32[]{:S(2)}) collective-permute-start(bf16[256,128]{1,0:T(8,128)(2,1)S(1)} %section.26.refs_0_), channel_id=1, source_target_pairs={{0,2},{1,3},{2,0},{3,1},{4,6},{5,7},{6,4},{7,5},{8,10},{9,11},{10,... | collective-permute-start | bytes 196616 | tf_op jit(solution)/shard_map/ppermute | solution.py:255
  23.9 5.9 %collective-permute-start.14 = (bf16[256,128]{1,0:T(8,128)(2,1)S(1)}, bf16[256,128]{1,0:T(8,128)(2,1)S(1)}, u32[]{:S(2)}, u32[]{:S(2)}) collective-permute-start(bf16[256,128]{1,0:T(8,128)(2,1)S(1)} %section.27.refs_0_), channel_id=1, source_target_pairs={{0,4},{1,5},{2,6},{3,7},{4,0},{5,1},{6,2},{7,3},{8,12},{9,13},{10,... | collective-permute-start | bytes 196616 | tf_op jit(solution)/shard_map/ppermute | solution.py:255
  25.9 7.0 %collective-permute-start.2 = (bf16[256,128]{1,0:T(8,128)(2,1)S(1)}, bf16[256,128]{1,0:T(8,128)(2,1)S(1)}, u32[]{:S(2)}, u32[]{:S(2)}) collective-permute-start(bf16[256,128]{1,0:T(8,128)(2,1)S(1)} %section.16.refs_0_), channel_id=1, source_target_pairs={{0,4},{1,5},{2,6},{3,7},{4,0},{5,1},{6,2},{7,3},{8,12},{9,13},{10,... | collective-permute-start | bytes 196616 | tf_op jit(solution)/shard_map/ppermute | solution.py:255
  26.5 14.4 %collective-permute-start.10 = (bf16[256,256]{1,0:T(8,128)(2,1)S(1)}, bf16[256,256]{1,0:T(8,128)(2,1)S(1)}, u32[]{:S(2)}, u32[]{:S(2)}) collective-permute-start(bf16[256,256]{1,0:T(8,128)(2,1)S(1)} %section.24.refs_0_), channel_id=1, source_target_pairs={{0,8},{1,9},{2,10},{3,11},{4,12},{5,13},{6,14},{7,15},{8,0},{9,1},... | collective-permute-start | bytes 393224 | tf_op jit(solution)/shard_map/ppermute | solution.py:255
  29.6 13.6 %collective-permute-start.6 = (bf16[256,256]{1,0:T(8,128)(2,1)S(1)}, bf16[256,256]{1,0:T(8,128)(2,1)S(1)}, u32[]{:S(2)}, u32[]{:S(2)}) collective-permute-start(bf16[256,256]{1,0:T(8,128)(2,1)S(1)} %section.20.refs_0_), channel_id=1, source_target_pairs={{0,8},{1,9},{2,10},{3,11},{4,12},{5,13},{6,14},{7,15},{8,0},{9,1},... | collective-permute-start | bytes 393224 | tf_op jit(solution)/shard_map/ppermute | solution.py:255
  30.0 15.0 %collective-permute-start.15 = (bf16[256,128]{1,0:T(8,128)(2,1)S(1)}, bf16[256,128]{1,0:T(8,128)(2,1)S(1)}, u32[]{:S(2)}, u32[]{:S(2)}) collective-permute-start(bf16[256,128]{1,0:T(8,128)(2,1)S(1)} %section.28.refs_0_), channel_id=1, source_target_pairs={{0,8},{1,9},{2,10},{3,11},{4,12},{5,13},{6,14},{7,15},{8,0},{9,1},... | collective-permute-start | bytes 196616 | tf_op jit(solution)/shard_map/ppermute | solution.py:255
  33.1 14.5 %copy-start.1 = (bf16[1,14,256,256]{3,2,1,0:T(8,128)(2,1)S(1)}, bf16[1,14,256,256]{3,2,1,0:T(8,128)(2,1)}, u32[]{:S(2)}) copy-start(bf16[1,14,256,256]{3,2,1,0:T(8,128)(2,1)} %weight_ref.20) | copy-start | bytes 5505028
  33.1 14.5 %copy-start.2 = (bf16[2048,256]{1,0:T(8,128)(2,1)S(1)}, bf16[2048,256]{1,0:T(8,128)(2,1)}, u32[]{:S(2)}) copy-start(bf16[2048,256]{1,0:T(8,128)(2,1)} %decoder_ref.1) | copy-start | bytes 3145732
  33.1 12.7 %collective-permute-start.3 = (bf16[256,128]{1,0:T(8,128)(2,1)S(1)}, bf16[256,128]{1,0:T(8,128)(2,1)S(1)}, u32[]{:S(2)}, u32[]{:S(2)}) collective-permute-start(bf16[256,128]{1,0:T(8,128)(2,1)S(1)} %section.17.refs_0_), channel_id=1, source_target_pairs={{0,8},{1,9},{2,10},{3,11},{4,12},{5,13},{6,14},{7,15},{8,0},{9,1},... | collective-permute-start | bytes 196616 | tf_op jit(solution)/shard_map/ppermute | solution.py:255
  41.0 9.9 %collective-permute-start.11 = (bf16[256,256]{1,0:T(8,128)(2,1)S(1)}, bf16[256,256]{1,0:T(8,128)(2,1)S(1)}, u32[]{:S(2)}, u32[]{:S(2)}) collective-permute-start(bf16[256,256]{1,0:T(8,128)(2,1)S(1)} %section.25.refs_0_), channel_id=1, source_target_pairs={{0,16},{16,0},{1,17},{17,1},{2,18},{18,2},{3,19},{19,3},{4,20},{20... | collective-permute-start | bytes 393224 | tf_op jit(solution)/shard_map/ppermute | solution.py:255
  43.4 9.1 %collective-permute-start.7 = (bf16[256,256]{1,0:T(8,128)(2,1)S(1)}, bf16[256,256]{1,0:T(8,128)(2,1)S(1)}, u32[]{:S(2)}, u32[]{:S(2)}) collective-permute-start(bf16[256,256]{1,0:T(8,128)(2,1)S(1)} %section.21.refs_0_), channel_id=1, source_target_pairs={{0,16},{16,0},{1,17},{17,1},{2,18},{18,2},{3,19},{19,3},{4,20},{20... | collective-permute-start | bytes 393224 | tf_op jit(solution)/shard_map/ppermute | solution.py:255
  45.3 4.3 %collective-permute-start.16 = (bf16[256,128]{1,0:T(8,128)(2,1)S(1)}, bf16[256,128]{1,0:T(8,128)(2,1)S(1)}, u32[]{:S(2)}, u32[]{:S(2)}) collective-permute-start(bf16[256,128]{1,0:T(8,128)(2,1)S(1)} %section.29.refs_0_), channel_id=1, source_target_pairs={{0,16},{16,0},{1,17},{17,1},{2,18},{18,2},{3,19},{19,3},{4,20},{20... | collective-permute-start | bytes 196616 | tf_op jit(solution)/shard_map/ppermute | solution.py:255
  46.0 7.2 %collective-permute-start.4 = (bf16[256,128]{1,0:T(8,128)(2,1)S(1)}, bf16[256,128]{1,0:T(8,128)(2,1)S(1)}, u32[]{:S(2)}, u32[]{:S(2)}) collective-permute-start(bf16[256,128]{1,0:T(8,128)(2,1)S(1)} %section.18.refs_0_), channel_id=1, source_target_pairs={{0,16},{16,0},{1,17},{17,1},{2,18},{18,2},{3,19},{19,3},{4,20},{20... | collective-permute-start | bytes 196616 | tf_op jit(solution)/shard_map/ppermute | solution.py:255
where the time goes:
time: 54.8 us; the launch traced here: 54.6 us
  starting transfers between devices  22 us (40%)
  waiting for transfers between devices  19.7 us (36%)
  Pallas kernels  12.6 us (23%)
    ppermute x17, starting transfers between devices, from_partner(): other = lax.ppermute(block, axis, [(i, i ^ 1 << bit) for i in range(count)])  22 us
    ppermute x17, waiting for transfers between devices, from_partner(): other = lax.ppermute(block, axis, [(i, i ^ 1 << bit) for i in range(count)])  19.7 us
    pallas_call x3, Pallas kernels, finish(): pl.pallas_call(functools.partial(finish_kernel, len(boxes), piece, held_p...  4.24 us
    pallas_call x15, Pallas kernels, section(): pl.pallas_call(functools.partial(section_kernel, bit, piece, earlier), ou...  3.34 us
    pallas_call x1, Pallas kernels, encode_head(): pl.pallas_call(functools.partial(head_kernel, pieces), out_shape=[jax.Sha...  2.37 us
  transfers between devices with their start and end apart: 17, of which 6 were waited for; matrix products, arithmetic and copies ran while one was open for 0% of the time, Pallas kernels for 14%

commit v1 on v0

--- a/solution.py
+++ b/solution.py
@@ -57,9 +57,14 @@
         early.append(fetch(encoder_hbm.at[span, :], encoder_ref.at[span, :], sems.at[0, part]))
         early.append(fetch(sources_hbm.at[span, pl.ds(lo, hi - lo)], near[0].at[span, :], sems.at[1, part]))
     later = [
-        fetch(sources_hbm.at[:, pl.ds(lo, hi - lo)], near[i].at[:, :], sems.at[2, i])
+        fetch(
+            sources_hbm.at[pl.ds(half * (rows * PARTS // 2), rows * PARTS // 2), pl.ds(lo, hi - lo)],
+            near[i].at[pl.ds(half * (rows * PARTS // 2), rows * PARTS // 2), :],
+            sems.at[2, 2 * i - 2 + half],
+        )
         for i, (lo, hi) in enumerate(pieces)
         if i
+        for half in range(2)
     ]
     total = None
     for part, span in enumerate(spans):
@@ -87,7 +92,7 @@
         out_specs=[VMEM] * (1 + len(widths)),
         scratch_shapes=[
             pltpu.VMEM((points, widths[0]), BF16),
-            pltpu.SemaphoreType.DMA((3, max(PARTS, len(pieces)))),
+            pltpu.SemaphoreType.DMA((3, max(PARTS, 2 * len(pieces)))),
         ],
         compiler_params=pltpu.CompilerParams(vmem_limit_bytes=24 * MIB),
         cost_estimate=cost(2 * points * size * widths[0], 2 * points * (size + columns)),

time: 54.8 us -> 54.8 us (level)
  no operation moved by 1% of the time
where the time goes in v1:
time: 54.8 us; the launch traced here: 54.7 us
  starting transfers between devices  22 us (40%)
  waiting for transfers between devices  19.7 us (36%)
  Pallas kernels  12.7 us (23%)
    ppermute x17, starting transfers between devices, from_partner(): other = lax.ppermute(block, axis, [(i, i ^ 1 << bit) for i in range(count)])  22 us
    ppermute x17, waiting for transfers between devices, from_partner(): other = lax.ppermute(block, axis, [(i, i ^ 1 << bit) for i in range(count)])  19.7 us
    pallas_call x3, Pallas kernels, finish(): pl.pallas_call(functools.partial(finish_kernel, len(boxes), piece, held_p...  4.24 us
    pallas_call x15, Pallas kernels, section(): pl.pallas_call(functools.partial(section_kernel, bit, piece, earlier), ou...  3.34 us
    pallas_call x1, Pallas kernels, encode_head(): pl.pallas_call(functools.partial(head_kernel, pieces), out_shape=[jax.Sha...  2.39 us
  transfers between devices with their start and end apart: 17, of which 6 were waited for; matrix products, arithmetic and copies ran while one was open for 0% of the time, Pallas kernels for 14%

profile of v1, /device:TPU:0, one launch (start us, length us, event | category | flops | bytes accessed | tf_op | source)
XLA Modules:
  0.0 54.7 jit_solution(12832273017365840534)
XLA Ops:
  0.0 0.0 copy-start
  0.0 2.4 %head.1 = (bf16[256,128]{1,0:T(8,128)(2,1)S(1)}, bf16[2048,256]{1,0:T(8,128)(2,1)S(1)}, bf16[2048,640]{1,0:T(8,128)(2,1)S(1)}) custom-call(bf16[2048,256]{1,0:T(8,128)(2,1)} %encoder_hbm.1, bf16[2048,768]{1,0:T(8,128)(2,1)} %sources_hbm.1), custom_call_target="tpu_custom_call" | custom-call | flops 134217728 | bytes 4194304 | tf_op jit(solution)/shard_map/head/pallas_call | solution.py:84
  2.4 1.0 %encode.1.refs_0_ = bf16[256,640]{1,0:T(8,128)(2,1)S(1)} custom-call(bf16[2048,256]{1,0:T(8,128)(2,1)S(1)} %get-tuple-element.8.encoder_ref, bf16[2048,640]{1,0:T(8,128)(2,1)S(1)} %get-tuple-element.9.sources_ref), custom_call_target="tpu_custom_call" | custom-call | flops 671088640 | bytes 2621440 | tf_op jit(solution)/shard_map/encode/pallas_call | solution.py:113
  3.4 0.6 %collective-permute-start = (bf16[256,640]{1,0:T(8,128)(2,1)S(1)}, bf16[256,640]{1,0:T(8,128)(2,1)S(1)}, u32[]{:S(2)}, u32[]{:S(2)}) collective-permute-start(bf16[256,640]{1,0:T(8,128)(2,1)S(1)} %encode.1.refs_0_), channel_id=1, source_target_pairs={{0,1},{1,0},{2,3},{3,2},{4,5},{5,4},{6,7},{7,6},{8,9},{9,8},{10,11... | collective-permute-start | bytes 983048 | tf_op jit(solution)/shard_map/ppermute | solution.py:260
  4.0 1.3 %collective-permute-done.refs_1_ = bf16[256,640]{1,0:T(8,128)(2,1)S(1)} collective-permute-done((bf16[256,640]{1,0:T(8,128)(2,1)S(1)}, bf16[256,640]{1,0:T(8,128)(2,1)S(1)}, u32[]{:S(2)}, u32[]{:S(2)}) %collective-permute-start) | collective-permute-done | bytes 327712 | tf_op jit(solution)/shard_map/ppermute | solution.py:260
  5.2 0.0 copy-done
  5.2 0.3 section.15.refs_0_
  5.5 2.9 %collective-permute-start.1 = (bf16[256,384]{1,0:T(8,128)(2,1)S(1)}, bf16[256,384]{1,0:T(8,128)(2,1)S(1)}, u32[]{:S(2)}, u32[]{:S(2)}) collective-permute-start(bf16[256,384]{1,0:T(8,128)(2,1)S(1)} %section.15.refs_0_), channel_id=1, source_target_pairs={{0,2},{1,3},{2,0},{3,1},{4,6},{5,7},{6,4},{7,5},{8,10},{9,11},{10,... | collective-permute-start | bytes 589832 | tf_op jit(solution)/shard_map/ppermute | solution.py:260
  8.5 0.2 section.22.refs_0_
  8.7 0.1 collective-permute-start.8
  8.8 0.1 collective-permute-start.12
  8.8 7.6 %collective-permute-done.8.refs_1_ = bf16[256,256]{1,0:T(8,128)(2,1)S(1)} collective-permute-done((bf16[256,256]{1,0:T(8,128)(2,1)S(1)}, bf16[256,256]{1,0:T(8,128)(2,1)S(1)}, u32[]{:S(2)}, u32[]{:S(2)}) %collective-permute-start.8) | collective-permute-done | bytes 131104 | tf_op jit(solution)/shard_map/ppermute | solution.py:260
  16.5 0.2 section.23.refs_0_
  16.7 1.9 %collective-permute-start.9 = (bf16[256,256]{1,0:T(8,128)(2,1)S(1)}, bf16[256,256]{1,0:T(8,128)(2,1)S(1)}, u32[]{:S(2)}, u32[]{:S(2)}) collective-permute-start(bf16[256,256]{1,0:T(8,128)(2,1)S(1)} %section.23.refs_0_), channel_id=1, source_target_pairs={{0,4},{1,5},{2,6},{3,7},{4,0},{5,1},{6,2},{7,3},{8,12},{9,13},{10,... | collective-permute-start | bytes 393224 | tf_op jit(solution)/shard_map/ppermute | solution.py:260
  18.6 0.0 collective-permute-done.1.refs_1_
  18.6 0.2 section.19.refs_0_
  18.8 0.0 copy-start.3
  18.8 0.3 collective-permute-start.5
  19.1 0.0 collective-permute-done.12.refs_1_
  19.1 0.2 section.26.refs_0_
  19.3 1.8 %collective-permute-start.13 = (bf16[256,128]{1,0:T(8,128)(2,1)S(1)}, bf16[256,128]{1,0:T(8,128)(2,1)S(1)}, u32[]{:S(2)}, u32[]{:S(2)}) collective-permute-start(bf16[256,128]{1,0:T(8,128)(2,1)S(1)} %section.26.refs_0_), channel_id=1, source_target_pairs={{0,2},{1,3},{2,0},{3,1},{4,6},{5,7},{6,4},{7,5},{8,10},{9,11},{10,... | collective-permute-start | bytes 196616 | tf_op jit(solution)/shard_map/ppermute | solution.py:260
  21.1 2.5 %collective-permute-done.13.refs_1_ = bf16[256,128]{1,0:T(8,128)(2,1)S(1)} collective-permute-done((bf16[256,128]{1,0:T(8,128)(2,1)S(1)}, bf16[256,128]{1,0:T(8,128)(2,1)S(1)}, u32[]{:S(2)}, u32[]{:S(2)}) %collective-permute-start.13) | collective-permute-done | bytes 65568 | tf_op jit(solution)/shard_map/ppermute | solution.py:260
  23.7 0.2 section.27.refs_0_
  23.9 1.9 %collective-permute-start.14 = (bf16[256,128]{1,0:T(8,128)(2,1)S(1)}, bf16[256,128]{1,0:T(8,128)(2,1)S(1)}, u32[]{:S(2)}, u32[]{:S(2)}) collective-permute-start(bf16[256,128]{1,0:T(8,128)(2,1)S(1)} %section.27.refs_0_), channel_id=1, source_target_pairs={{0,4},{1,5},{2,6},{3,7},{4,0},{5,1},{6,2},{7,3},{8,12},{9,13},{10,... | collective-permute-start | bytes 196616 | tf_op jit(solution)/shard_map/ppermute | solution.py:260
  25.8 0.2 section.16.refs_0_
  26.0 0.3 collective-permute-start.2
  26.2 0.0 collective-permute-done.9.refs_1_
  26.2 0.2 section.24.refs_0_
  26.5 2.9 %collective-permute-start.10 = (bf16[256,256]{1,0:T(8,128)(2,1)S(1)}, bf16[256,256]{1,0:T(8,128)(2,1)S(1)}, u32[]{:S(2)}, u32[]{:S(2)}) collective-permute-start(bf16[256,256]{1,0:T(8,128)(2,1)S(1)} %section.24.refs_0_), channel_id=1, source_target_pairs={{0,8},{1,9},{2,10},{3,11},{4,12},{5,13},{6,14},{7,15},{8,0},{9,1},... | collective-permute-start | bytes 393224 | tf_op jit(solution)/shard_map/ppermute | solution.py:260
  29.4 0.0 collective-permute-done.5.refs_1_
  29.4 0.2 section.20.refs_0_
  29.6 0.1 collective-permute-start.6
  29.8 0.0 copy-done.3
  29.8 0.0 collective-permute-done.14.refs_1_
  29.8 0.2 section.28.refs_0_
  30.0 2.9 %collective-permute-start.15 = (bf16[256,128]{1,0:T(8,128)(2,1)S(1)}, bf16[256,128]{1,0:T(8,128)(2,1)S(1)}, u32[]{:S(2)}, u32[]{:S(2)}) collective-permute-start(bf16[256,128]{1,0:T(8,128)(2,1)S(1)} %section.28.refs_0_), channel_id=1, source_target_pairs={{0,8},{1,9},{2,10},{3,11},{4,12},{5,13},{6,14},{7,15},{8,0},{9,1},... | collective-permute-start | bytes 196616 | tf_op jit(solution)/shard_map/ppermute | solution.py:260
  32.9 0.0 collective-permute-done.2.refs_1_
  32.9 0.2 section.17.refs_0_
  33.1 0.0 copy-start.1
  33.2 0.0 copy-start.2
  33.2 0.7 %collective-permute-start.3 = (bf16[256,128]{1,0:T(8,128)(2,1)S(1)}, bf16[256,128]{1,0:T(8,128)(2,1)S(1)}, u32[]{:S(2)}, u32[]{:S(2)}) collective-permute-start(bf16[256,128]{1,0:T(8,128)(2,1)S(1)} %section.17.refs_0_), channel_id=1, source_target_pairs={{0,8},{1,9},{2,10},{3,11},{4,12},{5,13},{6,14},{7,15},{8,0},{9,1},... | collective-permute-start | bytes 196616 | tf_op jit(solution)/shard_map/ppermute | solution.py:260
  33.9 6.9 %collective-permute-done.10.refs_1_ = bf16[256,256]{1,0:T(8,128)(2,1)S(1)} collective-permute-done((bf16[256,256]{1,0:T(8,128)(2,1)S(1)}, bf16[256,256]{1,0:T(8,128)(2,1)S(1)}, u32[]{:S(2)}, u32[]{:S(2)}) %collective-permute-start.10) | collective-permute-done | bytes 131104 | tf_op jit(solution)/shard_map/ppermute | solution.py:260
  40.8 0.2 section.25.refs_0_
  41.1 1.8 %collective-permute-start.11 = (bf16[256,256]{1,0:T(8,128)(2,1)S(1)}, bf16[256,256]{1,0:T(8,128)(2,1)S(1)}, u32[]{:S(2)}, u32[]{:S(2)}) collective-permute-start(bf16[256,256]{1,0:T(8,128)(2,1)S(1)} %section.25.refs_0_), channel_id=1, source_target_pairs={{0,16},{16,0},{1,17},{17,1},{2,18},{18,2},{3,19},{19,3},{4,20},{20... | collective-permute-start | bytes 393224 | tf_op jit(solution)/shard_map/ppermute | solution.py:260
  42.9 0.3 collective-permute-done.6.refs_1_
  43.2 0.2 section.21.refs_0_
  43.4 1.6 %collective-permute-start.7 = (bf16[256,256]{1,0:T(8,128)(2,1)S(1)}, bf16[256,256]{1,0:T(8,128)(2,1)S(1)}, u32[]{:S(2)}, u32[]{:S(2)}) collective-permute-start(bf16[256,256]{1,0:T(8,128)(2,1)S(1)} %section.21.refs_0_), channel_id=1, source_target_pairs={{0,16},{16,0},{1,17},{17,1},{2,18},{18,2},{3,19},{19,3},{4,20},{20... | collective-permute-start | bytes 393224 | tf_op jit(solution)/shard_map/ppermute | solution.py:260
  45.0 0.0 collective-permute-done.15.refs_1_
  45.1 0.2 section.29.refs_0_
  45.3 0.6 %collective-permute-start.16 = (bf16[256,128]{1,0:T(8,128)(2,1)S(1)}, bf16[256,128]{1,0:T(8,128)(2,1)S(1)}, u32[]{:S(2)}, u32[]{:S(2)}) collective-permute-start(bf16[256,128]{1,0:T(8,128)(2,1)S(1)} %section.29.refs_0_), channel_id=1, source_target_pairs={{0,16},{16,0},{1,17},{17,1},{2,18},{18,2},{3,19},{19,3},{4,20},{20... | collective-permute-start | bytes 196616 | tf_op jit(solution)/shard_map/ppermute | solution.py:260
  45.8 0.0 collective-permute-done.3.refs_1_
  45.9 0.2 section.18.refs_0_
  46.1 1.6 %collective-permute-start.4 = (bf16[256,128]{1,0:T(8,128)(2,1)S(1)}, bf16[256,128]{1,0:T(8,128)(2,1)S(1)}, u32[]{:S(2)}, u32[]{:S(2)}) collective-permute-start(bf16[256,128]{1,0:T(8,128)(2,1)S(1)} %section.18.refs_0_), channel_id=1, source_target_pairs={{0,16},{16,0},{1,17},{17,1},{2,18},{18,2},{3,19},{19,3},{4,20},{20... | collective-permute-start | bytes 196616 | tf_op jit(solution)/shard_map/ppermute | solution.py:260
  47.7 0.0 copy-done.1
  47.7 0.0 copy-done.2
  47.7 0.9 %operator.1.refs_2_ = bf16[2048,256]{1,0:T(8,128)(2,1)S(1)} custom-call(bf16[1,14,256,256]{3,2,1,0:T(8,128)(2,1)S(1)} %copy-done.1, bf16[2048,256]{1,0:T(8,128)(2,1)S(1)} %copy-done.2), custom_call_target="tpu_custom_call" | custom-call | flops 671088640 | bytes 4194304 | tf_op jit(solution)/shard_map/operator/pallas_call | solution.py:170
  48.6 1.0 %collective-permute-done.16.refs_1_ = bf16[256,128]{1,0:T(8,128)(2,1)S(1)} collective-permute-done((bf16[256,128]{1,0:T(8,128)(2,1)S(1)}, bf16[256,128]{1,0:T(8,128)(2,1)S(1)}, u32[]{:S(2)}, u32[]{:S(2)}) %collective-permute-start.16) | collective-permute-done | bytes 65568 | tf_op jit(solution)/shard_map/ppermute | solution.py:260
  49.6 1.4 %finish.3.refs_3_ = bf16[2048,768]{1,0:T(8,128)(2,1)} custom-call(bf16[2,256,256]{2,1,0:T(8,128)(2,1)S(1)} %pad_maximum_fusion.crossing_ref, bf16[256,128]{1,0:T(8,128)(2,1)S(1)} %section.29.refs_0_, bf16[256,128]{1,0:T(8,128)(2,1)S(1)} %collective-permute-done.16.refs_1_, bf16[2048,256]{1,0:T(8,128)(2,1)S(1)} %operator.1.refs_2_), custom_call_target="tpu_custom_call" | custom-call | flops 134217728 | bytes 524288 | tf_op jit(solution)/shard_map/finish/pallas_call | solution.py:244
  51.0 0.0 collective-permute-done.11.refs_1_
  51.0 1.5 %finish.4.refs_4_ = bf16[2048,768]{1,0:T(8,128)(2,1)} custom-call(bf16[2,256,256]{2,1,0:T(8,128)(2,1)S(1)} %pad_maximum_fusion.crossing_ref, bf16[256,256]{1,0:T(8,128)(2,1)S(1)} %section.25.refs_0_, bf16[256,256]{1,0:T(8,128)(2,1)S(1)} %collective-permute-done.11.refs_1_, bf16[2048,256]{1,0:T(8,128)(2,1)S(1)} %operator.1.refs_2_, ...), custom_call_target="tpu_custom_call", output_to_operand_aliasing={{}: (4, {})} | custom-call | flops 268435456 | bytes 1048576 | tf_op jit(solution)/shard_map/finish/pallas_call | solution.py:244
  52.5 0.0 collective-permute-done.7.refs_1_
  52.5 0.8 %hold.1.refs_3_ = bf16[2048,256]{1,0:T(8,128)(2,1)S(1)} custom-call(bf16[2,256,256]{2,1,0:T(8,128)(2,1)S(1)} %pad_maximum_fusion.crossing_ref, bf16[256,256]{1,0:T(8,128)(2,1)S(1)} %section.21.refs_0_, bf16[256,256]{1,0:T(8,128)(2,1)S(1)} %collective-permute-done.7.refs_1_, bf16[2048,256]{1,0:T(8,128)(2,1)S(1)} %operator.1.refs_2_), custom_call_target="tpu_custom_call" | custom-call | flops 268435456 | bytes 1048576 | tf_op jit(solution)/shard_map/hold/pallas_call | solution.py:220
  53.3 0.0 collective-permute-done.4.refs_1_
  53.3 1.4 %finish.5 = bf16[2048,768]{1,0:T(8,128)(2,1)} custom-call(bf16[2,256,256]{2,1,0:T(8,128)(2,1)S(1)} %pad_maximum_fusion.crossing_ref, bf16[256,128]{1,0:T(8,128)(2,1)S(1)} %section.18.refs_0_, bf16[256,128]{1,0:T(8,128)(2,1)S(1)} %collective-permute-done.4.refs_1_, bf16[2048,256]{1,0:T(8,128)(2,1)S(1)} %operator.1.refs_2_, ...), custom_call_target="tpu_custom_call", output_to_operand_aliasing={{}: (5, {})} | custom-call | flops 134217728 | bytes 524288 | tf_op jit(solution)/shard_map/finish/pallas_call | solution.py:244
  (2 shorter events, 0.0 us)
Async XLA Ops:
  0.0 5.2 %copy-start = (bf16[1,4,2,256,256]{4,3,2,1,0:T(8,128)(2,1)S(1)}, bf16[1,4,2,256,256]{4,3,2,1,0:T(8,128)(2,1)}, u32[]{:S(2)}) copy-start(bf16[1,4,2,256,256]{4,3,2,1,0:T(8,128)(2,1)} %weight_ref.31) | copy-start | bytes 3145732
  3.4 1.8 %collective-permute-start = (bf16[256,640]{1,0:T(8,128)(2,1)S(1)}, bf16[256,640]{1,0:T(8,128)(2,1)S(1)}, u32[]{:S(2)}, u32[]{:S(2)}) collective-permute-start(bf16[256,640]{1,0:T(8,128)(2,1)S(1)} %encode.1.refs_0_), channel_id=1, source_target_pairs={{0,1},{1,0},{2,3},{3,2},{4,5},{5,4},{6,7},{7,6},{8,9},{9,8},{10,11... | collective-permute-start | bytes 983048 | tf_op jit(solution)/shard_map/ppermute | solution.py:260
  5.5 13.0 %collective-permute-start.1 = (bf16[256,384]{1,0:T(8,128)(2,1)S(1)}, bf16[256,384]{1,0:T(8,128)(2,1)S(1)}, u32[]{:S(2)}, u32[]{:S(2)}) collective-permute-start(bf16[256,384]{1,0:T(8,128)(2,1)S(1)} %section.15.refs_0_), channel_id=1, source_target_pairs={{0,2},{1,3},{2,0},{3,1},{4,6},{5,7},{6,4},{7,5},{8,10},{9,11},{10,... | collective-permute-start | bytes 589832 | tf_op jit(solution)/shard_map/ppermute | solution.py:260
  8.7 7.8 %collective-permute-start.8 = (bf16[256,256]{1,0:T(8,128)(2,1)S(1)}, bf16[256,256]{1,0:T(8,128)(2,1)S(1)}, u32[]{:S(2)}, u32[]{:S(2)}) collective-permute-start(bf16[256,256]{1,0:T(8,128)(2,1)S(1)} %section.22.refs_0_), channel_id=1, source_target_pairs={{0,2},{1,3},{2,0},{3,1},{4,6},{5,7},{6,4},{7,5},{8,10},{9,11},{10,... | collective-permute-start | bytes 393224 | tf_op jit(solution)/shard_map/ppermute | solution.py:260
  8.8 10.3 %collective-permute-start.12 = (bf16[256,128]{1,0:T(8,128)(2,1)S(1)}, bf16[256,128]{1,0:T(8,128)(2,1)S(1)}, u32[]{:S(2)}, u32[]{:S(2)}) collective-permute-start(bf16[256,128]{1,0:T(8,128)(2,1)S(1)} %get-tuple-element.10.refs_0_), channel_id=1, source_target_pairs={{0,1},{1,0},{2,3},{3,2},{4,5},{5,4},{6,7},{7,6},{8,9},{9,8},{10,11... | collective-permute-start | bytes 196616 | tf_op jit(solution)/shard_map/ppermute | solution.py:260
  16.7 9.6 %collective-permute-start.9 = (bf16[256,256]{1,0:T(8,128)(2,1)S(1)}, bf16[256,256]{1,0:T(8,128)(2,1)S(1)}, u32[]{:S(2)}, u32[]{:S(2)}) collective-permute-start(bf16[256,256]{1,0:T(8,128)(2,1)S(1)} %section.23.refs_0_), channel_id=1, source_target_pairs={{0,4},{1,5},{2,6},{3,7},{4,0},{5,1},{6,2},{7,3},{8,12},{9,13},{10,... | collective-permute-start | bytes 393224 | tf_op jit(solution)/shard_map/ppermute | solution.py:260
  18.8 10.9 %copy-start.3 = (bf16[1,1,2,256,256]{4,3,2,1,0:T(8,128)(2,1)S(1)}, bf16[1,1,2,256,256]{4,3,2,1,0:T(8,128)(2,1)}, u32[]{:S(2)}) copy-start(bf16[1,1,2,256,256]{4,3,2,1,0:T(8,128)(2,1)} %param.9) | copy-start | bytes 786436
  18.8 10.6 %collective-permute-start.5 = (bf16[256,256]{1,0:T(8,128)(2,1)S(1)}, bf16[256,256]{1,0:T(8,128)(2,1)S(1)}, u32[]{:S(2)}, u32[]{:S(2)}) collective-permute-start(bf16[256,256]{1,0:T(8,128)(2,1)S(1)} %section.19.refs_0_), channel_id=1, source_target_pairs={{0,4},{1,5},{2,6},{3,7},{4,0},{5,1},{6,2},{7,3},{8,12},{9,13},{10,... | collective-permute-start | bytes 393224 | tf_op jit(solution)/shard_map/ppermute | solution.py:260
  19.3 4.3 %collective-permute-start.13 = (bf16[256,128]{1,0:T(8,128)(2,1)S(1)}, bf16[256,128]{1,0:T(8,128)(2,1)S(1)}, u32[]{:S(2)}, u32[]{:S(2)}) collective-permute-start(bf16[256,128]{1,0:T(8,128)(2,1)S(1)} %section.26.refs_0_), channel_id=1, source_target_pairs={{0,2},{1,3},{2,0},{3,1},{4,6},{5,7},{6,4},{7,5},{8,10},{9,11},{10,... | collective-permute-start | bytes 196616 | tf_op jit(solution)/shard_map/ppermute | solution.py:260
  23.9 5.9 %collective-permute-start.14 = (bf16[256,128]{1,0:T(8,128)(2,1)S(1)}, bf16[256,128]{1,0:T(8,128)(2,1)S(1)}, u32[]{:S(2)}, u32[]{:S(2)}) collective-permute-start(bf16[256,128]{1,0:T(8,128)(2,1)S(1)} %section.27.refs_0_), channel_id=1, source_target_pairs={{0,4},{1,5},{2,6},{3,7},{4,0},{5,1},{6,2},{7,3},{8,12},{9,13},{10,... | collective-permute-start | bytes 196616 | tf_op jit(solution)/shard_map/ppermute | solution.py:260
  26.0 7.0 %collective-permute-start.2 = (bf16[256,128]{1,0:T(8,128)(2,1)S(1)}, bf16[256,128]{1,0:T(8,128)(2,1)S(1)}, u32[]{:S(2)}, u32[]{:S(2)}) collective-permute-start(bf16[256,128]{1,0:T(8,128)(2,1)S(1)} %section.16.refs_0_), channel_id=1, source_target_pairs={{0,4},{1,5},{2,6},{3,7},{4,0},{5,1},{6,2},{7,3},{8,12},{9,13},{10,... | collective-permute-start | bytes 196616 | tf_op jit(solution)/shard_map/ppermute | solution.py:260
  26.5 14.4 %collective-permute-start.10 = (bf16[256,256]{1,0:T(8,128)(2,1)S(1)}, bf16[256,256]{1,0:T(8,128)(2,1)S(1)}, u32[]{:S(2)}, u32[]{:S(2)}) collective-permute-start(bf16[256,256]{1,0:T(8,128)(2,1)S(1)} %section.24.refs_0_), channel_id=1, source_target_pairs={{0,8},{1,9},{2,10},{3,11},{4,12},{5,13},{6,14},{7,15},{8,0},{9,1},... | collective-permute-start | bytes 393224 | tf_op jit(solution)/shard_map/ppermute | solution.py:260
  29.6 13.6 %collective-permute-start.6 = (bf16[256,256]{1,0:T(8,128)(2,1)S(1)}, bf16[256,256]{1,0:T(8,128)(2,1)S(1)}, u32[]{:S(2)}, u32[]{:S(2)}) collective-permute-start(bf16[256,256]{1,0:T(8,128)(2,1)S(1)} %section.20.refs_0_), channel_id=1, source_target_pairs={{0,8},{1,9},{2,10},{3,11},{4,12},{5,13},{6,14},{7,15},{8,0},{9,1},... | collective-permute-start | bytes 393224 | tf_op jit(solution)/shard_map/ppermute | solution.py:260
  30.0 15.0 %collective-permute-start.15 = (bf16[256,128]{1,0:T(8,128)(2,1)S(1)}, bf16[256,128]{1,0:T(8,128)(2,1)S(1)}, u32[]{:S(2)}, u32[]{:S(2)}) collective-permute-start(bf16[256,128]{1,0:T(8,128)(2,1)S(1)} %section.28.refs_0_), channel_id=1, source_target_pairs={{0,8},{1,9},{2,10},{3,11},{4,12},{5,13},{6,14},{7,15},{8,0},{9,1},... | collective-permute-start | bytes 196616 | tf_op jit(solution)/shard_map/ppermute | solution.py:260
  33.1 14.5 %copy-start.1 = (bf16[1,14,256,256]{3,2,1,0:T(8,128)(2,1)S(1)}, bf16[1,14,256,256]{3,2,1,0:T(8,128)(2,1)}, u32[]{:S(2)}) copy-start(bf16[1,14,256,256]{3,2,1,0:T(8,128)(2,1)} %weight_ref.20) | copy-start | bytes 5505028
  33.2 14.5 %copy-start.2 = (bf16[2048,256]{1,0:T(8,128)(2,1)S(1)}, bf16[2048,256]{1,0:T(8,128)(2,1)}, u32[]{:S(2)}) copy-start(bf16[2048,256]{1,0:T(8,128)(2,1)} %decoder_ref.1) | copy-start | bytes 3145732
  33.2 12.7 %collective-permute-start.3 = (bf16[256,128]{1,0:T(8,128)(2,1)S(1)}, bf16[256,128]{1,0:T(8,128)(2,1)S(1)}, u32[]{:S(2)}, u32[]{:S(2)}) collective-permute-start(bf16[256,128]{1,0:T(8,128)(2,1)S(1)} %section.17.refs_0_), channel_id=1, source_target_pairs={{0,8},{1,9},{2,10},{3,11},{4,12},{5,13},{6,14},{7,15},{8,0},{9,1},... | collective-permute-start | bytes 196616 | tf_op jit(solution)/shard_map/ppermute | solution.py:260
  41.1 9.9 %collective-permute-start.11 = (bf16[256,256]{1,0:T(8,128)(2,1)S(1)}, bf16[256,256]{1,0:T(8,128)(2,1)S(1)}, u32[]{:S(2)}, u32[]{:S(2)}) collective-permute-start(bf16[256,256]{1,0:T(8,128)(2,1)S(1)} %section.25.refs_0_), channel_id=1, source_target_pairs={{0,16},{16,0},{1,17},{17,1},{2,18},{18,2},{3,19},{19,3},{4,20},{20... | collective-permute-start | bytes 393224 | tf_op jit(solution)/shard_map/ppermute | solution.py:260
  43.4 9.1 %collective-permute-start.7 = (bf16[256,256]{1,0:T(8,128)(2,1)S(1)}, bf16[256,256]{1,0:T(8,128)(2,1)S(1)}, u32[]{:S(2)}, u32[]{:S(2)}) collective-permute-start(bf16[256,256]{1,0:T(8,128)(2,1)S(1)} %section.21.refs_0_), channel_id=1, source_target_pairs={{0,16},{16,0},{1,17},{17,1},{2,18},{18,2},{3,19},{19,3},{4,20},{20... | collective-permute-start | bytes 393224 | tf_op jit(solution)/shard_map/ppermute | solution.py:260
  45.3 4.3 %collective-permute-start.16 = (bf16[256,128]{1,0:T(8,128)(2,1)S(1)}, bf16[256,128]{1,0:T(8,128)(2,1)S(1)}, u32[]{:S(2)}, u32[]{:S(2)}) collective-permute-start(bf16[256,128]{1,0:T(8,128)(2,1)S(1)} %section.29.refs_0_), channel_id=1, source_target_pairs={{0,16},{16,0},{1,17},{17,1},{2,18},{18,2},{3,19},{19,3},{4,20},{20... | collective-permute-start | bytes 196616 | tf_op jit(solution)/shard_map/ppermute | solution.py:260
  46.1 7.2 %collective-permute-start.4 = (bf16[256,128]{1,0:T(8,128)(2,1)S(1)}, bf16[256,128]{1,0:T(8,128)(2,1)S(1)}, u32[]{:S(2)}, u32[]{:S(2)}) collective-permute-start(bf16[256,128]{1,0:T(8,128)(2,1)S(1)} %section.18.refs_0_), channel_id=1, source_target_pairs={{0,16},{16,0},{1,17},{17,1},{2,18},{18,2},{3,19},{19,3},{4,20},{20... | collective-permute-start | bytes 196616 | tf_op jit(solution)/shard_map/ppermute | solution.py:260
